TPU v7x, 32 devices: a whole 2x2x4 slice. The times are simulated.
32 devices in a mesh: dp: 8 (over z, y), tensor: 4 (over x, core).
Axes of the slice: x: 2, y: 2, z: 4, core: 2. Of those that a mesh axis runs over, the one named last changes fastest.
Arguments:
- tree_ids: int32 [8, 64], P('dp'), may hold values from 0 to 65535, as said below
- ancestors: int32 [8, 64, 64], P('dp'), may hold values from 0 to 1, as said below
- lengths: int32 [8], P('dp'), may hold values from 64 to 1024, as said below
- table: bfloat16 [65536, 4096], P('dp', 'tensor'), may hold values from -3 to 3
- gain: bfloat16 [4096], replicated, may hold values from 0.25 to 1.75
- w_query: bfloat16 [4096, 4096], P(None, 'tensor'), may hold values from -0.09375 to 0.09375
- w_kv: bfloat16 [2, 4096, 1024], P(None, None, 'tensor'), may hold values from -0.09375 to 0.09375
- w_out: bfloat16 [4096, 4096], P('tensor'), may hold values from -0.09375 to 0.09375
- key_cache: bfloat16 [8, 8, 1024, 128], P('dp', 'tensor'), may hold values from -480 to 480
- value_cache: bfloat16 [8, 8, 1024, 128], P('dp', 'tensor'), may hold values from -6 to 6
Outputs:
- layer_output: bfloat16 [512, 4096], P('dp', 'tensor')
Inputs may be any that keep to these rules, and one draw needn't show every extreme that they name: `tree_ids`: split the vocabulary into equal consecutive parts, one for each index of dp; of the nodes of the rows of one index of dp, at most 16 have ids in any one part, and exactly 16 in some part. Row n of each row's matrix marks node n and all its ancestors in that row's tree; node 0 is the root and every other node's parent has a smaller index. `lengths`: some row has all 1024 slots live.
All inputs are finite; a program needn't handle non-finite values.
Results may differ from a plain program's by a relative error of at most 0.004.
The roundings to bfloat16 on the way count: a program that leaves them out, or rounds other values in their place, can miss the bound.
Values may be sent and summed in bfloat16 or wider, within the bound.
A program may use at most 128 MiB of HBM per device.

v0:
```python
import math
import jax
import jax.numpy as jnp
from jax import lax
from jax.sharding import PartitionSpec as P

D = 4096
EPS = 1e-05
NEG = -1e30
THETA = 500000.0


def rotary(values, positions):
    half_dim = values.shape[-1] // 2
    freq_index = jnp.arange(half_dim, dtype=jnp.float32)
    inverse = jnp.exp(freq_index * (-2.0 * math.log(THETA) / values.shape[-1]))
    angles = positions[:, None] * inverse[None, :]
    cosine = jnp.cos(angles)[:, None, :]
    sine_part = jnp.sin(angles)[:, None, :]
    lower_half = values[..., :half_dim]
    upper_half = values[..., half_dim:]
    return jnp.concatenate(
        [
            lower_half * cosine - upper_half * sine_part,
            upper_half * cosine + lower_half * sine_part,
        ],
        axis=-1,
    )


def contract(left_side, right_side):
    return lax.dot_general(
        left_side, right_side, (((1,), (1,)), ((), ())), preferred_element_type=jnp.float32
    )


def to_groups(tensor_in, kv_heads, head_dim):
    row_count, node_count, width_all = tensor_in.shape
    per_group = width_all // (kv_heads * head_dim)
    grouped = tensor_in.reshape(row_count, node_count, kv_heads, per_group, head_dim).transpose(
        0, 2, 3, 1, 4
    )
    return grouped.reshape(row_count, kv_heads, per_group * node_count, head_dim)


def from_groups(tensor_in, node_count):
    row_count, kv_heads, group_rows, head_dim = tensor_in.shape
    grouped = tensor_in.reshape(row_count, kv_heads, group_rows // node_count, node_count, head_dim)
    return grouped.transpose(0, 3, 1, 2, 4).reshape(row_count, node_count, -1)


def attend(query_group, keys_tree, values_tree, keys_cache, values_cache, live_len, tree_mask):
    score_scale = keys_cache.shape[-1] ** (-0.5)
    slot_count = keys_cache.shape[0]
    cache_scores = contract(query_group, keys_cache) * score_scale
    columns = jnp.arange(slot_count, dtype=jnp.int32)
    cache_scores = jnp.where(columns[None, :] < live_len, cache_scores, NEG)
    tree_scores = contract(query_group, keys_tree) * score_scale
    groups = query_group.shape[0] // tree_mask.shape[0]
    tree_scores = jnp.where(jnp.tile(tree_mask, (groups, 1)) > 0, tree_scores, NEG)
    row_top = jnp.maximum(jnp.max(cache_scores, axis=1), jnp.max(tree_scores, axis=1))[:, None]
    cache_exp = jnp.exp(cache_scores - row_top)
    tree_exp = jnp.exp(tree_scores - row_top)
    denominator = jnp.sum(cache_exp, axis=1) + jnp.sum(tree_exp, axis=1)
    cache_weights = cache_exp.astype(jnp.bfloat16)
    weighted = jnp.dot(
        tree_exp.astype(jnp.bfloat16), values_tree, preferred_element_type=jnp.float32
    )
    weighted = weighted + jnp.dot(cache_weights, values_cache, preferred_element_type=jnp.float32)
    return (weighted / denominator[:, None]).astype(jnp.bfloat16)


def slot_ranks(owner_blocks):
    token_span = owner_blocks.shape[-1]
    positions_here = jnp.arange(token_span, dtype=jnp.int32)
    earlier = positions_here[None, :] < positions_here[:, None]
    same_owner = owner_blocks[..., :, None] == owner_blocks[..., None, :]
    return jnp.sum((same_owner & earlier).astype(jnp.int32), axis=-1)


def shards(tree_ids, ancestors, lengths, table, gain, w_query, w_kv, w_out, key_cache, value_cache):
    row_count, node_count = tree_ids.shape
    token_count = row_count * node_count
    head_dim = key_cache.shape[3]
    kv_local = key_cache.shape[1]
    all_ids = lax.all_gather(tree_ids, "dp", axis=0, tiled=True).reshape(-1)
    vocab_rows = table.shape[0]
    dp_count = lax.axis_size("dp")
    my_index = lax.axis_index("dp")
    capacity = 2 * ((token_count + dp_count - 1) // dp_count)
    block_ids = all_ids.reshape(dp_count, token_count)
    owner_blocks = block_ids // vocab_rows
    ranks = slot_ranks(owner_blocks)
    mine = owner_blocks == my_index
    slot_hit = mine[:, :, None] & (
        ranks[:, :, None] == jnp.arange(capacity, dtype=jnp.int32)[None, None, :]
    )
    token_place = jnp.arange(token_count, dtype=jnp.int32)[None, :, None]
    source_token = jnp.sum(jnp.where(slot_hit, token_place, 0), axis=1)
    slot_used = jnp.any(slot_hit, axis=1)
    source_ids = jnp.take_along_axis(block_ids, source_token, axis=1)
    source_offsets = jnp.clip(source_ids - my_index * vocab_rows, 0, vocab_rows - 1)
    slot_rows = jnp.take(table, source_offsets.reshape(-1), axis=0).reshape(
        dp_count, capacity, table.shape[1]
    )
    slot_rows = jnp.where(slot_used[:, :, None], slot_rows, jnp.zeros((), slot_rows.dtype))
    arrived = lax.all_to_all(slot_rows, "dp", split_axis=0, concat_axis=0, tiled=True)
    own_ids = tree_ids.reshape(-1)
    own_owner = own_ids // vocab_rows
    own_rank = slot_ranks(own_owner)
    flat_slot = own_owner * capacity + own_rank
    embedded = jnp.take(arrived.reshape(dp_count * capacity, table.shape[1]), flat_slot, axis=0)
    gain_full = gain.astype(jnp.float32)
    features = lax.all_gather(embedded, "tensor", axis=1, tiled=True).astype(jnp.float32)
    inv_rms = lax.rsqrt(jnp.sum(features * features, axis=1) / D + EPS)
    normed = (features * inv_rms[:, None] * gain_full[None, :]).astype(jnp.bfloat16)
    queries = jnp.dot(normed, w_query, preferred_element_type=jnp.float32)
    keys_new = jnp.dot(normed, w_kv[0], preferred_element_type=jnp.float32)
    values_raw = jnp.dot(normed, w_kv[1], preferred_element_type=jnp.float32)
    values_new = values_raw.astype(jnp.bfloat16).reshape(row_count, node_count, -1)
    node_depth = jnp.sum(ancestors, axis=2) - 1
    positions = (lengths[:, None] + node_depth).reshape(-1).astype(jnp.float32)
    query_heads = w_query.shape[1] // head_dim
    queries = rotary(queries.reshape(token_count, query_heads, head_dim), positions).astype(
        jnp.bfloat16
    )
    queries = queries.reshape(row_count, node_count, query_heads * head_dim)
    keys_new = rotary(keys_new.reshape(token_count, kv_local, head_dim), positions).astype(
        jnp.bfloat16
    )
    keys_new = keys_new.reshape(row_count, node_count, kv_local * head_dim)
    query_groups = to_groups(queries, kv_local, head_dim)
    key_groups = to_groups(keys_new, kv_local, head_dim)
    value_groups = to_groups(values_new, kv_local, head_dim)

    def per_row(row_items):
        row_q, row_k, row_v, row_kc, row_vc, live_len, tree_mask = row_items

        def per_head(head_items):
            return attend(
                head_items[0],
                head_items[1],
                head_items[2],
                head_items[3],
                head_items[4],
                live_len,
                tree_mask,
            )

        return lax.map(per_head, (row_q, row_k, row_v, row_kc, row_vc))

    contexts = lax.map(
        per_row,
        (query_groups, key_groups, value_groups, key_cache, value_cache, lengths, ancestors),
    )
    contexts = from_groups(contexts, node_count).reshape(token_count, query_heads * head_dim)
    partial_out = jnp.dot(contexts, w_out, preferred_element_type=jnp.float32)
    attention = lax.psum_scatter(partial_out, "tensor", scatter_dimension=1, tiled=True)
    return (embedded.astype(jnp.float32) + attention).astype(jnp.bfloat16)


def solution(mesh):
    in_specs = (
        P("dp", None),
        P("dp", None, None),
        P("dp"),
        P("dp", "tensor"),
        P(),
        P(None, "tensor"),
        P(None, None, "tensor"),
        P("tensor", None),
        P("dp", "tensor", None, None),
        P("dp", "tensor", None, None),
    )
    out_specs = P("dp", "tensor")
    return jax.shard_map(shards, mesh=mesh, in_specs=in_specs, out_specs=out_specs, check_vma=False)
```

profile of v0, /device:TPU:0, one launch (start us, length us, event | category | flops | bytes accessed | tf_op | source)
XLA Modules:
  0.0 113.7 jit_solution(4923900093917061358)
XLA Ops:
  6.5 0.0 copy-start.4
  6.5 22.5 %all-gather = s32[8,1,64]{2,1,0:T(1,128)S(1)} all-gather(s32[1,1,64]{2,1,0:T(1,128)} %bitcast.147), channel_id=1, replica_groups=mesh['dp'=8,'tensor'=4] {'dp'}, dimensions={0}, use_global_device_ids=true | all-gather | bytes 2304 | tf_op jit(solution)/shard_map/all_gather | solution.py:86
  29.0 0.3 convert_reduce_fusion
  29.4 0.2 select_reduce_fusion
  29.6 0.1 reduce_sum.73
  29.7 0.2 fusion.43
  29.9 0.1 reshape.421
  30.0 1.0 gather_fusion.2
  31.0 0.0 copy-start.2
  31.0 0.0 copy-start.3
  31.0 0.1 reshape.424
  31.1 9.0 %gather_fusion = bf16[128,1024]{1,0:T(8,128)(2,1)S(1)} fusion(bf16[8192,1024]{1,0:T(8,128)(2,1)} %param.15, s32[1024]{0:T(1024)S(1)} %pad_clamp_fusion.1), kind=kCustom, calls=%fused_computation | custom fusion | bytes 524800 | tf_op jit(solution)/shard_map/jit(_take)/gather | solution.py:103
  40.1 0.8 select_select_fusion
  41.0 3.4 %all-to-all-start = ((bf16[8,16,1024]{2,1,0:T(8,128)(2,1)}), bf16[8,16,1024]{2,1,0:T(8,128)(2,1)S(1)}, u32[]{:S(2)}, u32[]{:S(2)}) async-start(bf16[8,16,1024]{2,1,0:T(8,128)(2,1)} %select_select_fusion), calls=%async_computation | async-start | bytes 524288 | tf_op jit(solution)/shard_map/all_to_all | solution.py:107
  44.4 0.0 reduce-scatter.2.cloned.1.call-start
  44.4 0.0 copy-done.4
  44.5 0.2 convert_reduce_fusion.1
  44.7 3.1 %slice_bitcast_fusion = bf16[256,4096]{0,1:T(8,128)(2,1)} fusion(bf16[2,4096,256]{2,1,0:T(8,128)(2,1)} %param.18), kind=kLoop, calls=%fused_computation.42 | loop fusion | bytes 4194304 | tf_op jit(solution)/shard_map/dot_general | solution.py:118
  48.4 0.0 copy-done.2
  48.4 0.1 reduce_sum.76
  48.6 0.1 copy.29
  48.6 0.0 copy-done.3
  48.7 2.9 %copy.32 = bf16[256,4096]{1,0:T(8,128)(2,1)S(1)} copy(bf16[256,4096]{0,1:T(8,128)(2,1)} %slice_bitcast_fusion) | data formatting | bytes 4194304 | tf_op jit(solution)/shard_map/dot_general | solution.py:118
  51.6 0.2 multiply_cosine_fusion
  51.8 0.7 all-to-all-done
  52.5 0.7 gather_fusion.1
  53.2 0.1 broadcast_select_fusion
  53.3 7.2 %all_gather.7 = bf16[64,4096]{1,0:T(8,128)(2,1)S(1)} all-gather(bf16[64,1024]{1,0:T(8,128)(2,1)S(1)} %broadcast_select_fusion), channel_id=1, replica_groups=mesh['dp'=8,'tensor'=4] {'tensor'}, dimensions={1}, use_global_device_ids=true | all-gather | bytes 655360 | tf_op jit(solution)/shard_map/all_gather | solution.py:114
  60.5 0.2 fusion.37
  60.7 2.1 %fusion.34 = bf16[64,256]{1,0:T(8,128)(2,1)S(1)} fusion(bf16[2,4096,256]{2,1,0:T(8,128)(2,1)} %param.18, bf16[64,4096]{1,0:T(8,128)(2,1)S(1)} %all_gather.7, f32[4096]{0:T(1024)S(1)} %convert_element_type.60, f32[64]{0:T(128)S(1)} %add_rsqrt_fusion), kind=kOutput, calls=%fused_computation.46 | convolution fusion | flops 135282688 | bytes 2670848 | tf_op jit(solution)/shard_map/dot_general | solution.py:119
  62.8 0.8 fusion.40
  63.6 0.0 copy-start
  63.6 0.0 copy-start.1
  63.7 5.1 %convolution_bitcast_fusion = f32[8,8,8,128]{3,1,2,0:T(8,128)S(1)} fusion(bf16[4096,1024]{1,0:T(8,128)(2,1)} %param.17, bf16[64,4096]{1,0:T(8,128)(2,1)S(1)} %all_gather.7, f32[4096]{0:T(1024)S(1)} %convert_element_type.60, f32[64]{0:T(128)S(1)} %add_rsqrt_fusion), kind=kOutput, calls=%fused_computation.45 | convolution fusion | flops 537919488 | bytes 9191680 | tf_op jit(solution)/shard_map/dot_general | solution.py:117
  68.8 0.1 fusion.44
  68.9 0.2 subtract_convert_fusion
  69.1 0.1 pad_maximum_fusion
  69.2 0.1 maximum_bitcast_fusion
  69.3 0.0 copy-done
  69.3 0.0 copy-done.1
  69.4 4.8 %while.17 = (s32[]{:T(128)}, bf16[2,256,128]{2,1,0:T(8,128)(2,1)S(1)}, s32[64,64]{0,1:T(8,128)S(1)}, bf16[2,256,128]{2,1,0:T(8,128)(2,1)S(1)}, bf16[2,64,128]{2,...) while((s32[]{:T(128)}, ...), condition=%wide.region_11.12_spmd, body=%wide.region_6.11_spmd.sunk | while | flops 144658944 | bytes 4468845 | solution.py:150
  69.4 0.7 iota_compare_fusion.4
  70.0 0.4 fusion.79
  70.5 0.1 gt.11
  70.6 0.2 fusion.78
  70.8 0.3 fusion.81
  71.1 0.2 fusion.80
  71.3 0.4 fusion.83
  71.7 0.7 iota_compare_fusion.4
  72.4 0.4 fusion.79
  72.8 0.1 gt.11
  73.0 0.2 fusion.78
  73.2 0.3 fusion.81
  73.5 0.2 fusion.80
  73.7 0.4 fusion.83
  74.1 0.1 copy.38
  74.2 0.1 reshape_reshape.9
  74.3 5.9 %fusion.59 = f32[64,4096]{1,0:T(8,128)} fusion(bf16[64,1024]{1,0:T(8,128)(2,1)S(1)} %reshape_reshape.9, bf16[1024,4096]{1,0:T(8,128)(2,1)} %param.19), kind=kOutput, calls=%fused_computation.120 | convolution fusion | flops 536870912 | bytes 9568256 | tf_op jit(solution)/shard_map/dot_general | solution.py:157
  80.2 0.0 reduce-scatter.2.cloned.1.call-update
  80.3 24.9 %reduce-scatter.2.cloned.1.call-done = f32[64,1024]{1,0:T(8,128)} async-done(((f32[64,4096]{1,0:T(8,128)}), f32[64,1024]{1,0:T(8,128)}) %reduce-scatter.2.cloned.1.call-update) | async-done | bytes 262160 | tf_op jit(solution)/shard_map/reduce_scatter | solution.py:158
  105.1 1.7 %add_convert_fusion = bf16[64,1024]{1,0:T(8,128)(2,1)} fusion(f32[64,1024]{1,0:T(8,128)} %reduce-scatter.2.cloned.1.call-done, bf16[64,1024]{1,0:T(8,128)(2,1)S(1)} %gather_fusion.1, pred[64]{0:T(512)(128)(4,1)S(1)} %compare_and_fusion.1), kind=kLoop, calls=%fused_computation.52 | loop fusion | flops 262144 | bytes 524352 | tf_op jit(solution)/shard_map/convert_element_type | solution.py:159
  (30 shorter events, 0.4 us)
Async XLA Ops:
  6.5 37.9 %copy-start.4 = (s32[1,64]{1,0:T(1,128)S(1)}, s32[1,64]{1,0:T(1,128)}, u32[]{:S(2)}) copy-start(s32[1,64]{1,0:T(1,128)} %param.12) | copy-start | bytes 772
  31.0 17.4 %copy-start.2 = (s32[1,64,64]{2,1,0:T(8,128)S(1)}, s32[1,64,64]{2,1,0:T(8,128)}, u32[]{:S(2)}) copy-start(s32[1,64,64]{2,1,0:T(8,128)} %param.13) | copy-start | bytes 49156
  31.0 17.6 %copy-start.3 = (bf16[4096]{0:T(1024)(128)(2,1)S(1)}, bf16[4096]{0:T(1024)(128)(2,1)}, u32[]{:S(2)}) copy-start(bf16[4096]{0:T(1024)(128)(2,1)} %param.16) | copy-start | bytes 24580
  41.0 11.6 %all-to-all-start = ((bf16[8,16,1024]{2,1,0:T(8,128)(2,1)}), bf16[8,16,1024]{2,1,0:T(8,128)(2,1)S(1)}, u32[]{:S(2)}, u32[]{:S(2)}) async-start(bf16[8,16,1024]{2,1,0:T(8,128)(2,1)} %select_select_fusion), calls=%async_computation | async-start | bytes 524288 | tf_op jit(solution)/shard_map/all_to_all | solution.py:107
  44.4 60.8 %reduce-scatter.2.cloned.1.call-start = ((), (), s32[]{:S(2)}) async-start(), calls=%async_computation.2 | async-start | bytes 1310720 | tf_op jit(solution)/shard_map/reduce_scatter | solution.py:158
  63.6 5.7 %copy-start = (bf16[1,2,1024,128]{3,2,1,0:T(8,128)(2,1)S(1)}, bf16[1,2,1024,128]{3,2,1,0:T(8,128)(2,1)}, u32[]{:S(2)}) copy-start(bf16[1,2,1024,128]{3,2,1,0:T(8,128)(2,1)} %param.21) | copy-start | bytes 1572868
  63.6 5.7 %copy-start.1 = (bf16[1,2,1024,128]{3,2,1,0:T(8,128)(2,1)S(1)}, bf16[1,2,1024,128]{3,2,1,0:T(8,128)(2,1)}, u32[]{:S(2)}) copy-start(bf16[1,2,1024,128]{3,2,1,0:T(8,128)(2,1)} %param.20) | copy-start | bytes 1572868
Sparse Core Ops, SparseCore 0:
  80.4 24.6 reduce-scatter.1
where the time goes:
time: 114 us
  blocking collectives  29.6 us (26%)
  waiting for transfers between devices  25.6 us (22%)
  local copies, waits for them, and re-layouts  17.6 us (15%)
  matrix products  16.2 us (14%)
  between operations  14.3 us (13%)
  other arithmetic  6.69 us (6%)
  starting transfers between devices  3.45 us (3%)
    reduce_scatter x1, waiting for transfers between devices, shards(): lax.psum_scatter(partial_out, 'tensor', scatter_dimension=1, tiled=True)  24.9 us
    all_gather x1, blocking collectives, shards(): all_ids = lax.all_gather(tree_ids, 'dp', axis=0, tiled=True).reshape(-1)  22.5 us
    gather x1, local copies, waits for them, and re-layouts, shards(): jnp.take(table, source_offsets.reshape(-1), axis=0)  8.97 us
    all_gather x1, blocking collectives, shards(): lax.all_gather(embedded, 'tensor', axis=1, tiled=True).astype(jnp.float32)  7.17 us
    dot_general x2, local copies, waits for them, and re-layouts, shards(): keys_new = jnp.dot(normed, w_kv[0], preferred_element_type=jnp.float32)  6 us
    dot_general x1, matrix products, shards(): partial_out = jnp.dot(contexts, w_out, preferred_element_type=jnp.float32)  5.94 us
    dot_general x1, matrix products, shards(): queries = jnp.dot(normed, w_query, preferred_element_type=jnp.float32)  5.09 us
    all_to_all x1, starting transfers between devices, shards(): lax.all_to_all(slot_rows, 'dp', split_axis=0, concat_axis=0, tiled=True)  3.41 us
  transfers between devices with their start and end apart: 2, of which 2 were waited for; matrix products, arithmetic and copies ran while one was open for 6% of the time, Pallas kernels for 0%

commit v1 on v0

--- a/solution.py
+++ b/solution.py
@@ -8,6 +8,22 @@
 EPS = 1e-05
 NEG = -1e30
 THETA = 500000.0
+
+
+def write_the_slabs(shard_in, where_dim):
+    ndev = lax.axis_size("tensor")
+    queue = [(i0, (i0 + 1) % ndev) for i0 in range(ndev)]
+    items = [(i0, (i0 - 1) % ndev) for i0 in range(ndev)]
+    z2, main = ([shard_in], [shard_in])
+    for _ in range(ndev // 2):
+        last = lax.ppermute(z2[-1], "tensor", queue)
+        z2.append(last)
+    for _ in range((ndev - 1) // 2):
+        now = lax.ppermute(main[-1], "tensor", items)
+        main.append(now)
+    state_next = jnp.concatenate([*z2[::-1], *main[1:]], where_dim)
+    side_arr = lax.axis_index("tensor")
+    return jnp.roll(state_next, (side_arr - ndev // 2) * shard_in.shape[where_dim], where_dim)
 
 
 def rotary(values, positions):
@@ -111,7 +127,7 @@
     flat_slot = own_owner * capacity + own_rank
     embedded = jnp.take(arrived.reshape(dp_count * capacity, table.shape[1]), flat_slot, axis=0)
     gain_full = gain.astype(jnp.float32)
-    features = lax.all_gather(embedded, "tensor", axis=1, tiled=True).astype(jnp.float32)
+    features = write_the_slabs(embedded, 1).astype(jnp.float32)
     inv_rms = lax.rsqrt(jnp.sum(features * features, axis=1) / D + EPS)
     normed = (features * inv_rms[:, None] * gain_full[None, :]).astype(jnp.bfloat16)
     queries = jnp.dot(normed, w_query, preferred_element_type=jnp.float32)

time: 114 us -> 118 us (1.035)
  waiting for transfers between devices: 25.6 us -> 33.3 us
  blocking collectives: 29.6 us -> 22.5 us
  starting transfers between devices: 3.45 us -> 5.25 us
  matrix products: 16.2 us -> 17.5 us
    all_gather x1 -> x0, blocking collectives: 7.17 us -> none  [shards(): lax.all_gather(embedded, 'tensor', axis=1, tiled=True).astype(jnp.float32)]
    all_to_all x1, waiting for transfers between devices: 0.73 us -> 5.33 us  [shards(): lax.all_to_all(slot_rows, 'dp', split_axis=0, concat_axis=0, tiled=True)]
    ppermute x0 -> x3, waiting for transfers between devices: none -> 4.34 us  [the longest x2 3.95 us: write_the_slabs(): last = lax.ppermute(z2[-1], 'tensor', queue)]
    ppermute x0 -> x3, starting transfers between devices: none -> 1.8 us  [the longest x1 1.69 us: write_the_slabs(): now = lax.ppermute(main[-1], 'tensor', items)]
    dot_general x2, local copies, waits for them, and re-layouts: 6 us -> 4.66 us  [shards(): keys_new = jnp.dot(normed, w_kv[0], preferred_element_type=jnp.float32)]
    reduce_scatter x1, waiting for transfers between devices: 24.9 us -> 23.6 us  [shards(): lax.psum_scatter(partial_out, 'tensor', scatter_dimension=1, tiled=True)]
    dot_general x2, matrix products: 0.78 us -> 2 us  [attend(): jnp.dot(cache_weights, values_cache, preferred_element_type=jnp.float32)]
  transfers between devices with their start and end apart: 2 -> 5, of which waited for: 2 -> 5; matrix products, arithmetic and copies ran while one was open for 6% -> 5% of each run, Pallas kernels for 0% -> 0%
where the time goes in v1:
time: 118 us
  waiting for transfers between devices  33.3 us (28%)
  blocking collectives  22.5 us (19%)
  matrix products  17.5 us (15%)
  local copies, waits for them, and re-layouts  17.3 us (15%)
  between operations  14.4 us (12%)
  other arithmetic  7.49 us (6%)
  starting transfers between devices  5.25 us (4%)
    reduce_scatter x1, waiting for transfers between devices, shards(): lax.psum_scatter(partial_out, 'tensor', scatter_dimension=1, tiled=True)  23.6 us
    all_gather x1, blocking collectives, shards(): all_ids = lax.all_gather(tree_ids, 'dp', axis=0, tiled=True).reshape(-1)  22.5 us
    gather x1, local copies, waits for them, and re-layouts, shards(): jnp.take(table, source_offsets.reshape(-1), axis=0)  8.97 us
    dot_general x1, matrix products, shards(): partial_out = jnp.dot(contexts, w_out, preferred_element_type=jnp.float32)  5.94 us
    all_to_all x1, waiting for transfers between devices, shards(): lax.all_to_all(slot_rows, 'dp', split_axis=0, concat_axis=0, tiled=True)  5.33 us
    dot_general x1, matrix products, shards(): queries = jnp.dot(normed, w_query, preferred_element_type=jnp.float32)  5.09 us
    dot_general x2, local copies, waits for them, and re-layouts, shards(): keys_new = jnp.dot(normed, w_kv[0], preferred_element_type=jnp.float32)  4.66 us
    ppermute x2, waiting for transfers between devices, write_the_slabs(): last = lax.ppermute(z2[-1], 'tensor', queue)  3.95 us
  transfers between devices with their start and end apart: 5, of which 5 were waited for; matrix products, arithmetic and copies ran while one was open for 5% of the time, Pallas kernels for 0%

profile of v1, /device:TPU:0, one launch (start us, length us, event | category | flops | bytes accessed | tf_op | source)
XLA Modules:
  0.0 117.6 jit_solution(3881327868106190758)
XLA Ops:
  6.6 22.5 %all-gather = s32[8,1,64]{2,1,0:T(1,128)S(1)} all-gather(s32[1,1,64]{2,1,0:T(1,128)} %bitcast.147), channel_id=1, replica_groups=mesh['dp'=8,'tensor'=4] {'dp'}, dimensions={0}, use_global_device_ids=true | all-gather | bytes 2304 | tf_op jit(solution)/shard_map/all_gather | solution.py:102
  29.0 0.3 convert_reduce_fusion
  29.4 0.2 select_reduce_fusion
  29.6 0.1 reduce_sum.73
  29.7 0.2 fusion.43
  29.9 0.1 reshape.421
  30.0 1.0 gather_fusion.2
  31.0 0.0 copy-start.3
  31.0 0.1 reshape.424
  31.1 0.0 copy-start.4
  31.1 9.0 %gather_fusion = bf16[128,1024]{1,0:T(8,128)(2,1)S(1)} fusion(bf16[8192,1024]{1,0:T(8,128)(2,1)} %param.15, s32[1024]{0:T(1024)S(1)} %pad_clamp_fusion.1), kind=kCustom, calls=%fused_computation | custom fusion | bytes 524800 | tf_op jit(solution)/shard_map/jit(_take)/gather | solution.py:119
  40.1 0.8 select_select_fusion
  40.9 3.4 %all-to-all-start = ((bf16[8,16,1024]{2,1,0:T(8,128)(2,1)}), bf16[8,16,1024]{2,1,0:T(8,128)(2,1)S(1)}, u32[]{:S(2)}, u32[]{:S(2)}) async-start(bf16[8,16,1024]{2,1,0:T(8,128)(2,1)} %select_select_fusion), calls=%async_computation | async-start | bytes 524288 | tf_op jit(solution)/shard_map/all_to_all | solution.py:123
  44.3 0.0 reduce-scatter.2.cloned.1.call-start
  44.4 0.0 copy-done.5
  44.4 1.7 %slice_bitcast_fusion = bf16[256,4096]{0,1:T(8,128)(2,1)S(1)} fusion(bf16[2,4096,256]{2,1,0:T(8,128)(2,1)} %param.18), kind=kLoop, calls=%fused_computation.42 | loop fusion | bytes 4194304 | tf_op jit(solution)/shard_map/dot_general | solution.py:134
  46.8 0.2 convert_reduce_fusion.1
  47.0 0.1 reduce_sum.76
  47.2 5.3 %all-to-all-done = bf16[8,16,1024]{2,1,0:T(8,128)(2,1)S(1)} async-done(((bf16[8,16,1024]{2,1,0:T(8,128)(2,1)}), bf16[8,16,1024]{2,1,0:T(8,128)(2,1)S(1)}, u32[]{:S(2)}, u32[]{:S(2)}) %all-to-all-start) | async-done | bytes 262176 | tf_op jit(solution)/shard_map/all_to_all | solution.py:123
  52.5 0.7 gather_fusion.1
  53.2 0.7 broadcast_select_fusion
  53.9 0.0 collective-permute-start
  54.0 0.1 copy.29
  54.1 2.9 %copy.32 = bf16[256,4096]{1,0:T(8,128)(2,1)} copy(bf16[256,4096]{0,1:T(8,128)(2,1)S(1)} %slice_bitcast_fusion) | data formatting | bytes 4194304 | tf_op jit(solution)/shard_map/dot_general | solution.py:134
  57.0 1.6 %collective-permute-done = bf16[64,1024]{1,0:T(8,128)(2,1)S(1)} collective-permute-done((bf16[64,1024]{1,0:T(8,128)(2,1)}, bf16[64,1024]{1,0:T(8,128)(2,1)S(1)}, u32[]{:S(2)}, u32[]{:S(2)}) %collective-permute-start) | collective-permute-done | bytes 131104 | tf_op jit(solution)/shard_map/ppermute | solution.py:19
  58.6 0.1 collective-permute-start.1
  58.7 0.2 multiply_cosine_fusion
  58.9 1.7 %collective-permute-start.2 = (bf16[64,1024]{1,0:T(8,128)(2,1)}, bf16[64,1024]{1,0:T(8,128)(2,1)S(1)}, u32[]{:S(2)}, u32[]{:S(2)}) collective-permute-start(bf16[64,1024]{1,0:T(8,128)(2,1)} %broadcast_select_fusion), channel_id=1, source_target_pairs={{0,3},{1,0},{2,1},{3,2},{4,7},{5,4},{6,5},{7,6},{8,11},{9,8},{10,9... | collective-permute-start | bytes 393224 | tf_op jit(solution)/shard_map/ppermute | solution.py:22
  60.5 2.4 %collective-permute-done.1 = bf16[64,1024]{1,0:T(8,128)(2,1)S(1)} collective-permute-done((bf16[64,1024]{1,0:T(8,128)(2,1)S(1)}, bf16[64,1024]{1,0:T(8,128)(2,1)S(1)}, u32[]{:S(2)}, u32[]{:S(2)}) %collective-permute-start.1) | collective-permute-done | bytes 131104 | tf_op jit(solution)/shard_map/ppermute | solution.py:19
  63.0 0.1 constant_dynamic-update-slice_fusion.5
  63.1 0.4 collective-permute-done.2
  63.5 0.1 constant_dynamic-update-slice_fusion.1
  63.6 0.2 fusion.37
  63.9 2.1 %fusion.34 = bf16[64,256]{1,0:T(8,128)(2,1)S(1)} fusion(bf16[2,4096,256]{2,1,0:T(8,128)(2,1)} %param.18, f32[4096]{0:T(1024)S(1)} %convert_element_type.60, f32[64]{0:T(128)S(1)} %add_rsqrt_fusion, bf16[64,8192]{1,0:T(8,128)(2,1)S(1)} %constant_dynamic-update-slice_fusion, s32[]{:T(128)S(6)} %select_n.160), kind=kOutput, calls=%fused_computation.46 | convolution fusion | flops 135282688 | bytes 2671108 | tf_op jit(solution)/shard_map/dot_general | solution.py:135
  66.0 0.0 copy-done
  66.0 0.8 fusion.40
  66.8 0.0 copy-start.1
  66.8 0.0 copy-start.2
  66.8 5.1 %convolution_bitcast_fusion = f32[8,8,8,128]{3,1,2,0:T(8,128)S(1)} fusion(bf16[4096,1024]{1,0:T(8,128)(2,1)} %param.17, f32[4096]{0:T(1024)S(1)} %convert_element_type.60, f32[64]{0:T(128)S(1)} %add_rsqrt_fusion, bf16[64,8192]{1,0:T(8,128)(2,1)S(1)} %constant_dynamic-update-slice_fusion, s32[]{:T(128)S(6)} %select_n.160), kind=kOutput, calls=%fused_computation.45 | convolution fusion | flops 537919488 | bytes 9191940 | tf_op jit(solution)/shard_map/dot_general | solution.py:133
  72.0 0.1 fusion.44
  72.1 0.2 subtract_convert_fusion
  72.3 0.1 pad_maximum_fusion
  72.4 0.1 maximum_bitcast_fusion
  72.5 6.0 %while.17 = (s32[]{:T(128)}, bf16[2,256,128]{2,1,0:T(8,128)(2,1)}, s32[64,64]{0,1:T(8,128)S(1)}, bf16[2,256,128]{2,1,0:T(8,128)(2,1)S(1)}, bf16[2,64,128]{2,1,0:...) while((s32[]{:T(128)}, bf16[2,256,128]{2,1,0:T(8,128)(2,1)}, ...), condition=%wide.region_11.12_spmd, body=%wide.region_6.11_spmd.sunk | while | flops 144658944 | bytes 4468845 | solution.py:166
  72.5 0.7 iota_compare_fusion.4
  73.2 0.4 fusion.79
  73.6 0.1 gt.11
  73.8 0.2 fusion.78
  73.9 0.3 fusion.81
  74.3 0.2 fusion.80
  74.5 1.0 fusion.83
  75.5 0.6 iota_compare_fusion.4
  76.2 0.4 fusion.79
  76.6 0.1 gt.11
  76.7 0.2 fusion.78
  76.9 0.3 fusion.81
  77.3 0.2 fusion.80
  77.5 1.0 fusion.83
  78.5 1.0 copy.38
  79.5 0.1 reshape_reshape.9
  79.6 5.9 %fusion.59 = f32[64,4096]{1,0:T(8,128)} fusion(bf16[64,1024]{1,0:T(8,128)(2,1)S(1)} %reshape_reshape.9, bf16[1024,4096]{1,0:T(8,128)(2,1)} %param.19), kind=kOutput, calls=%fused_computation.128 | convolution fusion | flops 536870912 | bytes 9568256 | tf_op jit(solution)/shard_map/dot_general | solution.py:173
  85.5 0.0 reduce-scatter.2.cloned.1.call-update
  85.5 23.6 %reduce-scatter.2.cloned.1.call-done = f32[64,1024]{1,0:T(8,128)} async-done(((f32[64,4096]{1,0:T(8,128)}), f32[64,1024]{1,0:T(8,128)}) %reduce-scatter.2.cloned.1.call-update) | async-done | bytes 262160 | tf_op jit(solution)/shard_map/reduce_scatter | solution.py:174
  109.1 1.7 %add_convert_fusion = bf16[64,1024]{1,0:T(8,128)(2,1)} fusion(f32[64,1024]{1,0:T(8,128)} %reduce-scatter.2.cloned.1.call-done, bf16[64,1024]{1,0:T(8,128)(2,1)S(1)} %gather_fusion.1, pred[64]{0:T(512)(128)(4,1)S(1)} %compare_and_fusion.1), kind=kLoop, calls=%fused_computation.52 | loop fusion | flops 262144 | bytes 524352 | tf_op jit(solution)/shard_map/convert_element_type | solution.py:175
  (42 shorter events, 0.5 us)
Async XLA Ops:
  6.5 37.9 %copy-start.5 = (s32[1,64]{1,0:T(1,128)S(1)}, s32[1,64]{1,0:T(1,128)}, u32[]{:S(2)}) copy-start(s32[1,64]{1,0:T(1,128)} %param.12) | copy-start | bytes 772
  31.0 16.0 %copy-start.3 = (s32[1,64,64]{2,1,0:T(8,128)S(1)}, s32[1,64,64]{2,1,0:T(8,128)}, u32[]{:S(2)}) copy-start(s32[1,64,64]{2,1,0:T(8,128)} %param.13) | copy-start | bytes 49156
  31.1 22.9 %copy-start.4 = (bf16[4096]{0:T(1024)(128)(2,1)S(1)}, bf16[4096]{0:T(1024)(128)(2,1)}, u32[]{:S(2)}) copy-start(bf16[4096]{0:T(1024)(128)(2,1)} %param.16) | copy-start | bytes 24580
  40.9 11.6 %all-to-all-start = ((bf16[8,16,1024]{2,1,0:T(8,128)(2,1)}), bf16[8,16,1024]{2,1,0:T(8,128)(2,1)S(1)}, u32[]{:S(2)}, u32[]{:S(2)}) async-start(bf16[8,16,1024]{2,1,0:T(8,128)(2,1)} %select_select_fusion), calls=%async_computation | async-start | bytes 524288 | tf_op jit(solution)/shard_map/all_to_all | solution.py:123
  44.3 64.8 %reduce-scatter.2.cloned.1.call-start = ((), (), s32[]{:S(2)}) async-start(), calls=%async_computation.2 | async-start | bytes 1310720 | tf_op jit(solution)/shard_map/reduce_scatter | solution.py:174
  53.9 4.6 %collective-permute-start = (bf16[64,1024]{1,0:T(8,128)(2,1)}, bf16[64,1024]{1,0:T(8,128)(2,1)S(1)}, u32[]{:S(2)}, u32[]{:S(2)}) collective-permute-start(bf16[64,1024]{1,0:T(8,128)(2,1)} %broadcast_select_fusion), channel_id=1, source_target_pairs={{0,1},{1,2},{2,3},{3,0},{4,5},{5,6},{6,7},{7,4},{8,9},{9,10},{10,1... | collective-permute-start | bytes 393224 | tf_op jit(solution)/shard_map/ppermute | solution.py:19
  57.0 9.0 %copy-start = (bf16[256,4096]{1,0:T(8,128)(2,1)S(1)}, bf16[256,4096]{1,0:T(8,128)(2,1)}, u32[]{:S(2)}) copy-start(bf16[256,4096]{1,0:T(8,128)(2,1)} %copy.32) | copy-start | bytes 6291460
  58.6 4.4 %collective-permute-start.1 = (bf16[64,1024]{1,0:T(8,128)(2,1)S(1)}, bf16[64,1024]{1,0:T(8,128)(2,1)S(1)}, u32[]{:S(2)}, u32[]{:S(2)}) collective-permute-start(bf16[64,1024]{1,0:T(8,128)(2,1)S(1)} %collective-permute-done), channel_id=1, source_target_pairs={{0,1},{1,2},{2,3},{3,0},{4,5},{5,6},{6,7},{7,4},{8,9},{9,10},{10,1... | collective-permute-start | bytes 393224 | tf_op jit(solution)/shard_map/ppermute | solution.py:19
  58.9 4.6 %collective-permute-start.2 = (bf16[64,1024]{1,0:T(8,128)(2,1)}, bf16[64,1024]{1,0:T(8,128)(2,1)S(1)}, u32[]{:S(2)}, u32[]{:S(2)}) collective-permute-start(bf16[64,1024]{1,0:T(8,128)(2,1)} %broadcast_select_fusion), channel_id=1, source_target_pairs={{0,3},{1,0},{2,1},{3,2},{4,7},{5,4},{6,5},{7,6},{8,11},{9,8},{10,9... | collective-permute-start | bytes 393224 | tf_op jit(solution)/shard_map/ppermute | solution.py:22
  66.8 5.7 %copy-start.1 = (bf16[1,2,1024,128]{3,2,1,0:T(8,128)(2,1)S(1)}, bf16[1,2,1024,128]{3,2,1,0:T(8,128)(2,1)}, u32[]{:S(2)}) copy-start(bf16[1,2,1024,128]{3,2,1,0:T(8,128)(2,1)} %param.21) | copy-start | bytes 1572868
  66.8 5.7 %copy-start.2 = (bf16[1,2,1024,128]{3,2,1,0:T(8,128)(2,1)S(1)}, bf16[1,2,1024,128]{3,2,1,0:T(8,128)(2,1)}, u32[]{:S(2)}) copy-start(bf16[1,2,1024,128]{3,2,1,0:T(8,128)(2,1)} %param.20) | copy-start | bytes 1572868
Sparse Core Ops, SparseCore 0:
  85.6 23.4 reduce-scatter.1
